TPU v7x, 128 devices: a whole 4x4x4 slice. The times are simulated.
128 devices in a mesh: row: 16 (over z, x), col: 8 (over y, core).
Axes of the slice: x: 4, y: 4, z: 4, core: 2. Of those that a mesh axis runs over, the one named last changes fastest.
Arguments:
- child_front: bfloat16 [16, 4096, 1024], P('row', 'col'), may hold values from -6 to 6
- child_inverse: bfloat16 [16, 1024, 1024], P('row'), as said below
- child_index: int32 [16, 32], P('row'), may hold values from 0 to 79, as said below
- child_size: int32 [16], P('row'), may hold values from 4 to 32, as said below
- front: float32 [10240, 10240], P('row', 'col'), may hold values from -6 to 6
- panel_inverse: float32 [256, 256], replicated, as said below
Outputs:
- trailing: float32 [10240, 10240], P('row', 'col')
- panel_rows: float32 [10240, 256], P('row')
Inputs may be any that keep to these rules, and one draw needn't show every extreme that they name: `child_index`: for each child r, the entries t < child_size[r] are increasing root tile numbers; later entries are arbitrary tile numbers and are not used. Cutting the root tiles into aligned runs of 5 tiles, a child has at most 2 live tiles in any run, and exactly 2 in each of two neighbouring runs 2q and 2q + 1 for some q. `child_size`: some child has the smallest and some child the largest possible size in every draw. `child_inverse`: lower triangular with a positive diagonal. `panel_inverse`: lower triangular with a positive diagonal.
All inputs are finite; a program needn't handle non-finite values.
Results may differ from a plain program's by a relative error of at most 0.0034.
Values may be sent and summed in bfloat16 or wider, within the bound.
A program may use at most 128 MiB of HBM per device.

v0:
```python
import jax
import jax.numpy as jnp
from jax import lax
from jax.sharding import PartitionSpec as P

TILE = 128
PANEL = 256
BLOCK_TILES = 2


def from_root(value, axis, source):
    kept = jnp.where(lax.axis_index(axis) == source, value, 0).astype(value.dtype)
    return lax.psum(kept, axis)


def slot_tiles(tile_index, first_slot, slot_count, slot_width, base_tile, sentinel):
    positions = jnp.arange(slot_width, dtype=jnp.int32)
    picked = jnp.take(tile_index, jnp.clip(first_slot + positions, 0, tile_index.shape[0] - 1))
    return jnp.where(positions < slot_count, picked - base_tile, sentinel)


def shards(child_front, child_inverse, child_index, child_size, front, panel_inverse):
    precise = lax.Precision.HIGHEST
    rows_dev = front.shape[0]
    cols_dev = front.shape[1]
    tiles_row = rows_dev // TILE
    tiles_col = cols_dev // TILE
    blocks = lax.axis_size("row")
    column = lax.axis_index("col")
    double = 2 * BLOCK_TILES
    factor_part = lax.dot_general(
        child_front[0],
        child_inverse[0],
        (((1,), (1,)), ((), ())),
        preferred_element_type=jnp.float32,
    ).astype(jnp.bfloat16)
    factor = lax.all_gather(factor_part, "col", axis=0, tiled=True)
    tile_index = child_index[0]
    live_tiles = jnp.arange(tile_index.shape[0], dtype=jnp.int32) < child_size[0]
    row_owner = jnp.where(live_tiles, tile_index // tiles_row, blocks)
    targets = jnp.arange(blocks, dtype=jnp.int32)
    starts = jnp.sum((row_owner[None, :] < targets[:, None]).astype(jnp.int32), axis=1)
    counts = jnp.sum((row_owner[None, :] == targets[:, None]).astype(jnp.int32), axis=1)
    col_owner = jnp.where(live_tiles, tile_index // tiles_col, lax.axis_size("col"))
    col_start = jnp.sum((col_owner < column).astype(jnp.int32))
    col_count = jnp.sum((col_owner == column).astype(jnp.int32))
    padded = jnp.concatenate(
        [factor, jnp.zeros((double * TILE, factor.shape[1]), factor.dtype)], axis=0
    )

    def row_rows(first_tile):
        return lax.dynamic_slice_in_dim(padded, first_tile * TILE, BLOCK_TILES * TILE, 0)

    def row_slots(first_tile, tile_count, target):
        return slot_tiles(
            tile_index, first_tile, tile_count, BLOCK_TILES, target * tiles_row, tiles_row
        )

    row_parts = jax.vmap(row_rows)(starts)
    col_part = lax.dynamic_slice_in_dim(padded, col_start * TILE, double * TILE, 0)
    row_targets = jax.vmap(row_slots)(starts, counts, targets)
    col_targets = slot_tiles(
        tile_index, col_start, col_count, double, column * tiles_col, tiles_col
    )
    col_sent = jnp.broadcast_to(col_targets[None, :], (blocks, double))
    width = padded.shape[1]
    row_tiles = row_parts.reshape(blocks, BLOCK_TILES, TILE, width)
    col_tiles = col_part.reshape(double, TILE, width)
    contribution = -jnp.einsum(
        "ikap,jbp->ikjab", row_tiles, col_tiles, preferred_element_type=jnp.float32
    )
    arrived, arrived_rows, arrived_cols = (
        lax.all_to_all(contribution, "row", split_axis=0, concat_axis=0, tiled=True),
        lax.all_to_all(row_targets, "row", split_axis=0, concat_axis=0, tiled=True),
        lax.all_to_all(col_sent, "row", split_axis=0, concat_axis=0, tiled=True),
    )
    tiled = front.reshape(tiles_row, TILE, tiles_col, TILE)
    tiled = tiled.at[arrived_rows[:, :, None], :, arrived_cols[:, None, :], :].add(
        arrived, mode="drop"
    )
    assembled = tiled.reshape(rows_dev, cols_dev)
    own_panel = lax.dot_general(
        assembled[:, :PANEL], panel_inverse, (((1,), (1,)), ((), ())), precision=precise
    )
    panel_rows = from_root(own_panel, "col", 0)
    whole_panel = lax.all_gather(panel_rows, "row", axis=0, tiled=True)
    across = lax.dynamic_slice_in_dim(whole_panel, column * cols_dev, cols_dev, 0)
    trailing = assembled - lax.dot_general(
        panel_rows, across, (((1,), (1,)), ((), ())), precision=precise
    )
    return (trailing, panel_rows)


def solution(mesh):
    in_specs = (
        P("row", "col", None),
        P("row", None, None),
        P("row", None),
        P("row"),
        P("row", "col"),
        P(),
    )
    out_specs = (P("row", "col"), P("row", None))
    return jax.shard_map(shards, mesh=mesh, in_specs=in_specs, out_specs=out_specs, check_vma=False)
```

profile of v0, /device:TPU:1, one launch (start us, length us, event | category | flops | bytes accessed | tf_op | source)
XLA Modules:
  0.0 468.3 jit_solution(3586415045492164564)
XLA Ops:
  8.8 3.5 fusion.2
  14.7 8.4 %all-to-all-start = ((s32[16,1,2]{2,1,0:T(1,128)}), s32[16,1,2]{2,1,0:T(1,128)S(1)}, u32[]{:S(2)}, u32[]{:S(2)}) async-start(s32[16,1,2]{2,1,0:T(1,128)} %bitcast.3), calls=%async_computation | async-start | bytes 16384 | tf_op jit(solution)/shard_map/all_to_all | solution.py:74
  27.2 38.6 %all-gather.3.cloned.1.call-done = bf16[4096,1024]{1,0:T(8,128)(2,1)} async-done(((bf16[512,1024]{1,0:T(8,128)(2,1)}), bf16[4096,1024]{1,0:T(8,128)(2,1)}) %all-gather.3.cloned.1.call-update) | async-done | bytes 8388624 | tf_op jit(solution)/shard_map/all_gather | solution.py:37
  65.7 8.0 %concatenate.10 = bf16[4608,1024]{1,0:T(8,128)(2,1)} pad(bf16[4096,1024]{1,0:T(8,128)(2,1)} %all-gather.3.cloned.1.call-done, bf16[]{:T(256)} %constant.41.clone.1), padding=0_512x0_0 | pad | bytes 17825794 | tf_op jit(solution)/shard_map/concatenate | solution.py:47
  73.7 51.5 %while.1 = (s32[]{:T(128)}, bf16[4608,1024]{1,0:T(8,128)(2,1)}, s32[16,2]{0,1:T(2,128)S(1)}, bf16[16,256,1024]{2,1,0:T(8,128)(2,1)}, s32[]{:T(128)}) while((s32[]{:T(128)}, bf16[4608,1024]{1,0:T(8,128)(2,1)}, s32[16,2]{0,1:T(2,128)S(1)}, bf16[16,256,1024]{2,1,0:T(8,128)(2,1)}, s32[]{:T(128)}) %tuple.22), condition=%wide.while_cond, body=%wide.while_body.sunk | while | flops 2 | bytes 1049689 | solution.py:52
  74.3 2.6 bitcast_dynamic-update-slice_fusion.2
  77.6 2.6 bitcast_dynamic-update-slice_fusion.2
  80.8 2.6 bitcast_dynamic-update-slice_fusion.2
  84.0 2.6 bitcast_dynamic-update-slice_fusion.2
  87.2 2.6 bitcast_dynamic-update-slice_fusion.2
  90.4 2.6 bitcast_dynamic-update-slice_fusion.2
  93.6 2.6 bitcast_dynamic-update-slice_fusion.2
  96.8 2.6 bitcast_dynamic-update-slice_fusion.2
  100.0 2.6 bitcast_dynamic-update-slice_fusion.2
  103.3 2.6 bitcast_dynamic-update-slice_fusion.2
  106.5 2.6 bitcast_dynamic-update-slice_fusion.2
  109.7 2.6 bitcast_dynamic-update-slice_fusion.2
  116.1 2.7 bitcast_dynamic-update-slice_fusion.2
  119.4 2.7 bitcast_dynamic-update-slice_fusion.2
  122.6 2.7 bitcast_dynamic-update-slice_fusion.2
  127.5 6.7 %all-to-all-start.1 = ((s32[16,1,4]{2,1,0:T(1,128)}), s32[16,1,4]{2,1,0:T(1,128)S(1)}, u32[]{:S(2)}, u32[]{:S(2)}) async-start(s32[16,1,4]{2,1,0:T(1,128)} %broadcast_in_dim.64), calls=%async_computation.1 | async-start | bytes 16384 | tf_op jit(solution)/shard_map/all_to_all | solution.py:75
  134.2 7.0 %negate_bitcast_fusion = f32[16,2,4,128,128]{3,4,1,0,2:T(8,128)S(1)} fusion(bf16[4,128,1024,1,1]{2,1,4,3,0:T(8,128)(2,1)S(1)} %bitcast.66, bf16[16,2,128,1024,1]{3,2,1,0,4:T(8,128)(2,1)} %bitcast.67), kind=kOutput, calls=%fused_computation.5 | convolution fusion | flops 4297064448 | bytes 17825792 | tf_op jit(solution)/shard_map/ikap,jbp->ikjab/dot_general | solution.py:69
  141.2 3.8 copy.40
  145.0 7.0 %all-to-all-start.2 = ((f32[16,2,4,128,128]{3,4,1,2,0:T(8,128)}), f32[16,2,4,128,128]{3,4,1,2,0:T(8,128)}, u32[]{:S(2)}, u32[]{:S(2)}) async-start(f32[16,2,4,128,128]{3,4,1,2,0:T(8,128)} %copy.40), calls=%async_computation.2 | async-start | bytes 16777216 | tf_op jit(solution)/shard_map/all_to_all | solution.py:73
  152.2 2.9 reshape.279
  155.1 3.5 copy.42
  159.4 115.5 %all-to-all-done.2 = f32[16,2,4,128,128]{3,4,1,2,0:T(8,128)} async-done(((f32[16,2,4,128,128]{3,4,1,2,0:T(8,128)}), f32[16,2,4,128,128]{3,4,1,2,0:T(8,128)}, u32[]{:S(2)}, u32[]{:S(2)}) %all-to-all-start.2) | async-done | bytes 8388640 | tf_op jit(solution)/shard_map/all_to_all | solution.py:73
  274.9 9.2 %copy.41 = f32[16,2,4,128,128]{4,3,2,1,0:T(8,128)} copy(f32[16,2,4,128,128]{3,4,1,2,0:T(8,128)} %all-to-all-done.2) | data formatting | bytes 16777216 | tf_op jit(solution)/shard_map/all_to_all | solution.py:73
  284.1 19.2 %scatter_fusion = f32[5,128,10,128]{3,1,2,0:T(8,128)S(1)} fusion(f32[5,128,10,128]{3,1,2,0:T(8,128)S(1)} %copy.42, s32[128]{0:T(128)S(1)} %reshape.318, f32[128,128,128]{2,1,0:T(8,128)} %bitcast.62), kind=kCustom, calls=%fused_computation.2 | custom fusion | flops 2097152 | bytes 25166848 | tf_op jit(solution)/shard_map/scatter-add | solution.py:78
  310.3 59.8 %all-reduce.4.cloned.1.call-done = f32[640,256]{1,0:T(8,128)} async-done(((f32[640,256]{1,0:T(8,128)}), f32[640,256]{1,0:T(8,128)}) %all-reduce.4.cloned.1.call-update) | async-done | bytes 655376 | tf_op jit(solution)/shard_map/psum | solution.py:13
  370.1 83.8 %all-gather.5.cloned.1.call-done = f32[10240,256]{1,0:T(8,128)} async-done(((f32[640,256]{1,0:T(8,128)}), f32[10240,256]{1,0:T(8,128)}) %all-gather.5.cloned.1.call-update) | async-done | bytes 10485776 | tf_op jit(solution)/shard_map/all_gather | solution.py:86
  453.8 7.0 %convolution_subtract_fusion = f32[640,1280]{1,0:T(8,128)} fusion(f32[640,1280]{1,0:T(8,128)} %bitcast.65, f32[640,256]{1,0:T(8,128)} %all-reduce.4.cloned.1.call-done, f32[10240,256]{1,0:T(8,128)} %all-gather.5.cloned.1.call-done, s32[]{:T(128)S(6)} %select_n.153), kind=kOutput, calls=%fused_computation.6 | convolution fusion | flops 2517401600 | bytes 8519684 | tf_op jit(solution)/shard_map/dot_general | solution.py:88
  (91 shorter events, 29.7 us)
Async XLA Ops:
  7.2 1.6 copy-start
  7.2 5.7 %copy-start.2 = (s32[1,32]{1,0:T(1,128)S(1)}, s32[1,32]{1,0:T(1,128)}, u32[]{:S(2)}) copy-start(s32[1,32]{1,0:T(1,128)} %param.8) | copy-start | bytes 388
  7.2 58.5 %all-gather.3.cloned.1.call-start = ((), (), s32[]{:S(2)}) async-start(), calls=%async_computation.3 | async-start | bytes 9437184 | tf_op jit(solution)/shard_map/all_gather | solution.py:37
  14.7 112.2 %all-to-all-start = ((s32[16,1,2]{2,1,0:T(1,128)}), s32[16,1,2]{2,1,0:T(1,128)S(1)}, u32[]{:S(2)}, u32[]{:S(2)}) async-start(s32[16,1,2]{2,1,0:T(1,128)} %bitcast.3), calls=%async_computation | async-start | bytes 16384 | tf_op jit(solution)/shard_map/all_to_all | solution.py:74
  127.5 17.5 %all-to-all-start.1 = ((s32[16,1,4]{2,1,0:T(1,128)}), s32[16,1,4]{2,1,0:T(1,128)S(1)}, u32[]{:S(2)}, u32[]{:S(2)}) async-start(s32[16,1,4]{2,1,0:T(1,128)} %broadcast_in_dim.64), calls=%async_computation.1 | async-start | bytes 16384 | tf_op jit(solution)/shard_map/all_to_all | solution.py:75
  145.0 7.2 %copy-start.5 = (f32[640,1280]{1,0:T(8,128)S(1)}, f32[640,1280]{1,0:T(8,128)}, u32[]{:S(2)}) copy-start(f32[640,1280]{1,0:T(8,128)} %param.10) | copy-start | bytes 9830404
  145.0 129.9 %all-to-all-start.2 = ((f32[16,2,4,128,128]{3,4,1,2,0:T(8,128)}), f32[16,2,4,128,128]{3,4,1,2,0:T(8,128)}, u32[]{:S(2)}, u32[]{:S(2)}) async-start(f32[16,2,4,128,128]{3,4,1,2,0:T(8,128)} %copy.40), calls=%async_computation.2 | async-start | bytes 16777216 | tf_op jit(solution)/shard_map/all_to_all | solution.py:73
  152.0 218.1 %all-reduce.4.cloned.1.call-start = ((), (), s32[]{:S(2)}) async-start(), calls=%async_computation.4 | async-start | bytes 1310720 | tf_op jit(solution)/shard_map/psum | solution.py:13
  303.3 5.3 %copy-start.6 = (f32[256,256]{1,0:T(8,128)S(1)}, f32[256,256]{1,0:T(8,128)}, u32[]{:S(2)}) copy-start(f32[256,256]{1,0:T(8,128)} %param.11) | copy-start | bytes 786436
  305.3 156.4 %copy-start.1 = (bf16[1,1024,1024]{2,1,0:T(8,128)(2,1)S(1)}, bf16[1,1024,1024]{2,1,0:T(8,128)(2,1)}, u32[]{:S(2)}) copy-start(bf16[1,1024,1024]{2,1,0:T(8,128)(2,1)} %param.7) | copy-start | bytes 6291460
  306.9 1.7 copy-start.3
  310.2 143.6 %all-gather.5.cloned.1.call-start = ((), (), s32[]{:S(2)}) async-start(), calls=%async_computation.5 | async-start | bytes 11141120 | tf_op jit(solution)/shard_map/all_gather | solution.py:86
  370.0 90.9 %copy-start.4 = (f32[640,256]{1,0:T(8,128)S(1)}, f32[640,256]{1,0:T(8,128)}, u32[]{:S(2)}) copy-start(f32[640,256]{1,0:T(8,128)} %all-reduce.4.cloned.1.call-done) | copy-start | bytes 1966084
Sparse Core Ops, SparseCore 0:
  12.4 53.2 all-gather.2
  310.4 59.6 all-reduce.3
  372.2 81.6 all-gather.4
where the time goes:
time: 470 us; the launch traced here: 468 us
  waiting for transfers between devices  298 us (63%)
  local copies, waits for them, and re-layouts  91 us (19%)
  other arithmetic  22.9 us (5%)
  starting transfers between devices  22.4 us (5%)
  matrix products  19.1 us (4%)
  between operations  15.3 us (3%)
    all_to_all x1, waiting for transfers between devices, shards(): lax.all_to_all(contribution, 'row', split_axis=0, concat_axis=0, tiled=True)  115 us
    all_gather x1, waiting for transfers between devices, shards(): whole_panel = lax.all_gather(panel_rows, 'row', axis=0, tiled=True)  83.8 us
    psum x1, waiting for transfers between devices, from_root(): return lax.psum(kept, axis)  59.8 us
    gather x48, local copies, waits for them, and re-layouts  51.5 us
    all_gather x1, waiting for transfers between devices, shards(): factor = lax.all_gather(factor_part, 'col', axis=0, tiled=True)  38.6 us
    scatter-add x1, other arithmetic, shards(): tiled.at[arrived_rows[:, :, None], :, arrived_cols[:, None, :], :]  19.2 us
  transfers between devices with their start and end apart: 6, of which 4 were waited for; matrix products, arithmetic and copies ran while one was open for 18% of the time, Pallas kernels for 0%

commit v1 on v0

--- a/solution.py
+++ b/solution.py
@@ -10,7 +10,7 @@
 
 def from_root(value, axis, source):
     kept = jnp.where(lax.axis_index(axis) == source, value, 0).astype(value.dtype)
-    return lax.psum(kept, axis)
+    return jnp.sum(lax.all_gather(kept, axis), axis=0)
 
 
 def slot_tiles(tile_index, first_slot, slot_count, slot_width, base_tile, sentinel):

time: 470 us -> 447 us (0.951)
  waiting for transfers between devices: 298 us -> 271 us
    psum x1 -> x0, waiting for transfers between devices: 59.8 us -> none  [from_root(): return lax.psum(kept, axis)]
    all_gather x0 -> x1, waiting for transfers between devices: none -> 37.2 us  [from_root(): return jnp.sum(lax.all_gather(kept, axis), axis=0)]
  transfers between devices with their start and end apart: 6 -> 6, of which waited for: 4 -> 4; matrix products, arithmetic and copies ran while one was open for 18% -> 19% of each run, Pallas kernels for 0% -> 0%
where the time goes in v1:
time: 447 us; the launch traced here: 445 us
  waiting for transfers between devices  271 us (61%)
  local copies, waits for them, and re-layouts  90.2 us (20%)
  other arithmetic  26.6 us (6%)
  starting transfers between devices  22.3 us (5%)
  matrix products  19 us (4%)
  between operations  15.3 us (3%)
    all_to_all x1, waiting for transfers between devices, shards(): lax.all_to_all(contribution, 'row', split_axis=0, concat_axis=0, tiled=True)  115 us
    all_gather x1, waiting for transfers between devices, shards(): whole_panel = lax.all_gather(panel_rows, 'row', axis=0, tiled=True)  80.1 us
    gather x48, local copies, waits for them, and re-layouts  51.6 us
    all_gather x1, waiting for transfers between devices, shards(): factor = lax.all_gather(factor_part, 'col', axis=0, tiled=True)  38.5 us
    all_gather x1, waiting for transfers between devices, from_root(): return jnp.sum(lax.all_gather(kept, axis), axis=0)  37.2 us
    scatter-add x1, other arithmetic, shards(): tiled.at[arrived_rows[:, :, None], :, arrived_cols[:, None, :], :]  19.2 us
    all_to_all x1, local copies, waits for them, and re-layouts, shards(): lax.all_to_all(contribution, 'row', split_axis=0, concat_axis=0, tiled=True)  9.25 us
  transfers between devices with their start and end apart: 6, of which 4 were waited for; matrix products, arithmetic and copies ran while one was open for 19% of the time, Pallas kernels for 0%

profile of v1, /device:TPU:1, one launch (start us, length us, event | category | flops | bytes accessed | tf_op | source)
XLA Modules:
  0.0 445.0 jit_solution(7186081504494665653)
XLA Ops:
  8.8 3.5 fusion.2
  14.7 8.4 %all-to-all-start = ((s32[16,1,2]{2,1,0:T(1,128)}), s32[16,1,2]{2,1,0:T(1,128)S(1)}, u32[]{:S(2)}, u32[]{:S(2)}) async-start(s32[16,1,2]{2,1,0:T(1,128)} %bitcast.3), calls=%async_computation | async-start | bytes 16384 | tf_op jit(solution)/shard_map/all_to_all | solution.py:74
  27.2 38.5 %all-gather.5.cloned.1.call-done = bf16[4096,1024]{1,0:T(8,128)(2,1)} async-done(((bf16[512,1024]{1,0:T(8,128)(2,1)}), bf16[4096,1024]{1,0:T(8,128)(2,1)}) %all-gather.5.cloned.1.call-update) | async-done | bytes 8388624 | tf_op jit(solution)/shard_map/all_gather | solution.py:37
  65.7 8.0 %concatenate.10 = bf16[4608,1024]{1,0:T(8,128)(2,1)} pad(bf16[4096,1024]{1,0:T(8,128)(2,1)} %all-gather.5.cloned.1.call-done, bf16[]{:T(256)} %constant.41.clone.1), padding=0_512x0_0 | pad | bytes 17825794 | tf_op jit(solution)/shard_map/concatenate | solution.py:47
  73.7 51.6 %while.1 = (s32[]{:T(128)}, bf16[4608,1024]{1,0:T(8,128)(2,1)}, s32[16,2]{0,1:T(2,128)S(1)}, bf16[16,256,1024]{2,1,0:T(8,128)(2,1)}, s32[]{:T(128)}) while((s32[]{:T(128)}, bf16[4608,1024]{1,0:T(8,128)(2,1)}, s32[16,2]{0,1:T(2,128)S(1)}, bf16[16,256,1024]{2,1,0:T(8,128)(2,1)}, s32[]{:T(128)}) %tuple.22), condition=%wide.while_cond, body=%wide.while_body.sunk | while | flops 2 | bytes 1049689 | solution.py:52
  74.3 2.6 bitcast_dynamic-update-slice_fusion.2
  77.6 2.6 bitcast_dynamic-update-slice_fusion.2
  80.8 2.6 bitcast_dynamic-update-slice_fusion.2
  84.0 2.6 bitcast_dynamic-update-slice_fusion.2
  90.4 2.6 bitcast_dynamic-update-slice_fusion.2
  93.6 2.6 bitcast_dynamic-update-slice_fusion.2
  96.8 2.6 bitcast_dynamic-update-slice_fusion.2
  100.1 2.6 bitcast_dynamic-update-slice_fusion.2
  103.3 2.6 bitcast_dynamic-update-slice_fusion.2
  106.5 2.6 bitcast_dynamic-update-slice_fusion.2
  109.7 2.6 bitcast_dynamic-update-slice_fusion.2
  116.2 2.7 bitcast_dynamic-update-slice_fusion.2
  119.4 2.7 bitcast_dynamic-update-slice_fusion.2
  122.7 2.7 bitcast_dynamic-update-slice_fusion.2
  127.6 6.7 %all-to-all-start.1 = ((s32[16,1,4]{2,1,0:T(1,128)}), s32[16,1,4]{2,1,0:T(1,128)S(1)}, u32[]{:S(2)}, u32[]{:S(2)}) async-start(s32[16,1,4]{2,1,0:T(1,128)} %broadcast_in_dim.64), calls=%async_computation.1 | async-start | bytes 16384 | tf_op jit(solution)/shard_map/all_to_all | solution.py:75
  134.3 7.0 %negate_bitcast_fusion = f32[16,2,4,128,128]{3,4,1,0,2:T(8,128)S(1)} fusion(bf16[4,128,1024,1,1]{2,1,4,3,0:T(8,128)(2,1)S(1)} %bitcast.68, bf16[16,2,128,1024,1]{3,2,1,0,4:T(8,128)(2,1)} %bitcast.69), kind=kOutput, calls=%fused_computation.5 | convolution fusion | flops 4297064448 | bytes 17825792 | tf_op jit(solution)/shard_map/ikap,jbp->ikjab/dot_general | solution.py:69
  141.2 3.8 copy.40
  145.1 7.0 %all-to-all-start.2 = ((f32[16,2,4,128,128]{3,4,1,2,0:T(8,128)}), f32[16,2,4,128,128]{3,4,1,2,0:T(8,128)}, u32[]{:S(2)}, u32[]{:S(2)}) async-start(f32[16,2,4,128,128]{3,4,1,2,0:T(8,128)} %copy.40), calls=%async_computation.2 | async-start | bytes 16777216 | tf_op jit(solution)/shard_map/all_to_all | solution.py:73
  152.3 2.9 reshape.279
  155.2 3.5 copy.42
  159.5 115.5 %all-to-all-done.2 = f32[16,2,4,128,128]{3,4,1,2,0:T(8,128)} async-done(((f32[16,2,4,128,128]{3,4,1,2,0:T(8,128)}), f32[16,2,4,128,128]{3,4,1,2,0:T(8,128)}, u32[]{:S(2)}, u32[]{:S(2)}) %all-to-all-start.2) | async-done | bytes 8388640 | tf_op jit(solution)/shard_map/all_to_all | solution.py:73
  275.0 9.2 %copy.41 = f32[16,2,4,128,128]{4,3,2,1,0:T(8,128)} copy(f32[16,2,4,128,128]{3,4,1,2,0:T(8,128)} %all-to-all-done.2) | data formatting | bytes 16777216 | tf_op jit(solution)/shard_map/all_to_all | solution.py:73
  284.2 19.2 %scatter_fusion = f32[5,128,10,128]{3,1,2,0:T(8,128)S(1)} fusion(f32[5,128,10,128]{3,1,2,0:T(8,128)S(1)} %copy.42, s32[128]{0:T(128)S(1)} %reshape.318, f32[128,128,128]{2,1,0:T(8,128)} %bitcast.63), kind=kCustom, calls=%fused_computation.2 | custom fusion | flops 2097152 | bytes 25166848 | tf_op jit(solution)/shard_map/scatter-add | solution.py:78
  310.3 37.2 %all-gather.9.cloned.1.call-done = f32[5120,256]{1,0:T(8,128)} async-done(((f32[640,256]{1,0:T(8,128)}), f32[5120,256]{1,0:T(8,128)}) %all-gather.9.cloned.1.call-update) | async-done | bytes 5242896 | tf_op jit(solution)/shard_map/all_gather | solution.py:13
  347.5 3.7 reduce_sum.49
  351.3 80.1 %all-gather.7.cloned.1.call-done = f32[10240,256]{1,0:T(8,128)} async-done(((f32[640,256]{1,0:T(8,128)}), f32[10240,256]{1,0:T(8,128)}) %all-gather.7.cloned.1.call-update) | async-done | bytes 10485776 | tf_op jit(solution)/shard_map/all_gather | solution.py:86
  431.4 7.0 %convolution_subtract_fusion = f32[640,1280]{1,0:T(8,128)} fusion(f32[640,1280]{1,0:T(8,128)} %bitcast.66, f32[640,256]{1,0:T(8,128)} %reduce_sum.49, f32[10240,256]{1,0:T(8,128)} %all-gather.7.cloned.1.call-done, s32[]{:T(128)S(6)} %select_n.153), kind=kOutput, calls=%fused_computation.6 | convolution fusion | flops 2517401600 | bytes 8519684 | tf_op jit(solution)/shard_map/dot_general | solution.py:88
  (89 shorter events, 31.4 us)
Async XLA Ops:
  7.2 1.6 copy-start
  7.2 5.7 %copy-start.2 = (s32[1,32]{1,0:T(1,128)S(1)}, s32[1,32]{1,0:T(1,128)}, u32[]{:S(2)}) copy-start(s32[1,32]{1,0:T(1,128)} %param.8) | copy-start | bytes 388
  7.2 58.5 %all-gather.5.cloned.1.call-start = ((), (), s32[]{:S(2)}) async-start(), calls=%async_computation.3 | async-start | bytes 9437184 | tf_op jit(solution)/shard_map/all_gather | solution.py:37
  14.7 112.3 %all-to-all-start = ((s32[16,1,2]{2,1,0:T(1,128)}), s32[16,1,2]{2,1,0:T(1,128)S(1)}, u32[]{:S(2)}, u32[]{:S(2)}) async-start(s32[16,1,2]{2,1,0:T(1,128)} %bitcast.3), calls=%async_computation | async-start | bytes 16384 | tf_op jit(solution)/shard_map/all_to_all | solution.py:74
  127.6 17.5 %all-to-all-start.1 = ((s32[16,1,4]{2,1,0:T(1,128)}), s32[16,1,4]{2,1,0:T(1,128)S(1)}, u32[]{:S(2)}, u32[]{:S(2)}) async-start(s32[16,1,4]{2,1,0:T(1,128)} %broadcast_in_dim.64), calls=%async_computation.1 | async-start | bytes 16384 | tf_op jit(solution)/shard_map/all_to_all | solution.py:75
  145.1 7.2 %copy-start.4 = (f32[640,1280]{1,0:T(8,128)S(1)}, f32[640,1280]{1,0:T(8,128)}, u32[]{:S(2)}) copy-start(f32[640,1280]{1,0:T(8,128)} %param.10) | copy-start | bytes 9830404
  145.1 129.9 %all-to-all-start.2 = ((f32[16,2,4,128,128]{3,4,1,2,0:T(8,128)}), f32[16,2,4,128,128]{3,4,1,2,0:T(8,128)}, u32[]{:S(2)}, u32[]{:S(2)}) async-start(f32[16,2,4,128,128]{3,4,1,2,0:T(8,128)} %copy.40), calls=%async_computation.2 | async-start | bytes 16777216 | tf_op jit(solution)/shard_map/all_to_all | solution.py:73
  152.0 195.5 %all-gather.9.cloned.1.call-start = ((), (), s32[]{:S(2)}) async-start(), calls=%async_computation.5 | async-start | bytes 5898240 | tf_op jit(solution)/shard_map/all_gather | solution.py:13
  303.4 5.3 %copy-start.5 = (f32[256,256]{1,0:T(8,128)S(1)}, f32[256,256]{1,0:T(8,128)}, u32[]{:S(2)}) copy-start(f32[256,256]{1,0:T(8,128)} %param.11) | copy-start | bytes 786436
  307.0 1.7 copy-start.3
  307.0 131.5 %copy-start.1 = (bf16[1,1024,1024]{2,1,0:T(8,128)(2,1)S(1)}, bf16[1,1024,1024]{2,1,0:T(8,128)(2,1)}, u32[]{:S(2)}) copy-start(bf16[1,1024,1024]{2,1,0:T(8,128)(2,1)} %param.7) | copy-start | bytes 6291460
  310.3 121.1 %all-gather.7.cloned.1.call-start = ((), (), s32[]{:S(2)}) async-start(), calls=%async_computation.4 | async-start | bytes 11141120 | tf_op jit(solution)/shard_map/all_gather | solution.py:86
Sparse Core Ops, SparseCore 0:
  12.4 53.2 all-gather.4
  310.4 37.0 all-gather.8
  351.4 79.9 all-gather.6
